TPU v7x, 32 devices: a whole 2x2x4 slice. The times are simulated.
32 devices in a mesh: ctx: 8 (over z, core), head: 4 (over y, x).
Axes of the slice: x: 2, y: 2, z: 4, core: 2. Of those that a mesh axis runs over, the one named last changes fastest.
Arguments:
- query_rows: bfloat16 [8192, 512], P('ctx', 'head'), may hold values from -0.5 to 0.5
- key_rows: bfloat16 [8192, 512], P('ctx', 'head'), may hold values from -0.5 to 0.5
- value_rows: bfloat16 [8192, 512], P('ctx', 'head'), may hold values from -40 to 40, as said below
- gate_logits: bfloat16 [8192, 512], P('ctx', 'head'), may hold values from -8 to 8
- log_decay: float32 [8192, 4], P('ctx', 'head'), may hold values from -1.2 to 0, as said below
- norm_gain: float32 [512], P('head'), may hold values from 0.1 to 1.9
- state_in: float32 [4, 128, 128], P('head'), may hold values from -256 to 256
- cotangent: bfloat16 [8192, 512], P('ctx', 'head'), may hold values from -6 to 6
- regroup: int32 [64], replicated, may hold values from 0 to 63, as said below
Outputs:
- gated_out: bfloat16 [8192, 512], P('ctx', 'head')
- grad_query: bfloat16 [8192, 512], P('ctx', 'head')
- grad_key: bfloat16 [8192, 512], P('ctx', 'head')
- grad_value: bfloat16 [8192, 512], P('ctx', 'head')
- grad_gate: bfloat16 [8192, 512], P('ctx', 'head')
Inputs may be any that keep to these rules, and one draw needn't show every extreme that they name: `value_rows`: values of order one per entry times a column and a row factor. `log_decay`: never positive. `regroup`: a permutation of the 64 pieces; the 8 places held by one device's 1024 tokens take exactly one piece from each device's 1024 tokens.
All inputs are finite; a program needn't handle non-finite values.
Results may differ from a plain program's by a relative error of at most 0.012.
Values may be sent and summed in bfloat16 or wider, within the bound.
A program may use at most 64 MiB of HBM per device.

v0:
```python
import jax
import jax.numpy as jnp
from jax import lax
from jax.sharding import PartitionSpec as P

BLOCK = 1024


exact_mode = lax.Precision.HIGHEST


def carried_in(shard, axis, join, neutral, backward):
    count = lax.axis_size(axis)
    place = lax.axis_index(axis)
    ahead = count - 1 - place if backward else place
    gathered = jax.tree.map(
        lambda a, kind: lax.all_gather(a.astype(kind), axis), shard, (jnp.bfloat16, jnp.bfloat16)
    )
    state = jax.tree.map(lambda a, e: jnp.zeros_like(a) + jnp.asarray(e, a.dtype), shard, neutral)

    def one(hop, state):
        source = count - 1 - hop if backward else hop
        return join(
            state,
            jax.tree.map(
                lambda a, own: lax.dynamic_index_in_dim(a, source, 0, False).astype(own.dtype),
                gathered,
                shard,
            ),
        )

    return lax.fori_loop(0, ahead, one, state)


def block_forward(kv_state, inputs):
    query_blk, key_blk, value_blk, decay_blk = inputs
    count = query_blk.shape[0]
    cum_log = jnp.cumsum(decay_blk, axis=0)
    positions = jnp.arange(count)
    causal = positions[:, None] >= positions[None, :]
    head_log = cum_log.T
    spread = jnp.where(causal[None], head_log[:, :, None] - head_log[:, None, :], 0.0)
    decay_mask = jnp.where(causal[None], jnp.exp(spread), 0.0)
    scores = jnp.einsum("thd,jhd->htj", query_blk, key_blk, preferred_element_type=jnp.float32)
    attn_probs = (scores * decay_mask).astype(jnp.bfloat16)
    within = jnp.einsum("htj,jhd->thd", attn_probs, value_blk, preferred_element_type=jnp.float32)
    carried = jnp.exp(cum_log)[:, :, None] * jnp.einsum(
        "thd,hde->the", query_blk.astype(jnp.float32), kv_state, precision=exact_mode
    )
    block_total = cum_log[-1]
    tail_weight = jnp.exp(block_total[None, :] - cum_log)
    update = jnp.einsum(
        "thd,the->hde",
        key_blk.astype(jnp.float32) * tail_weight[:, :, None],
        value_blk.astype(jnp.float32),
        precision=exact_mode,
    )
    next_state = jnp.exp(block_total)[:, None, None] * kv_state + update
    return (next_state, (within + carried, attn_probs, decay_mask, cum_log, kv_state))


def block_backward(grad_state, inputs):
    query_blk, key_blk, value_blk, grad_blk, attn_probs, decay_mask, cum_log, kv_state = inputs
    block_total = cum_log[-1]
    tail_weight = jnp.exp(block_total[None, :] - cum_log)[:, :, None]
    rise = jnp.exp(cum_log)[:, :, None]
    broad_derivative_matrix = grad_blk.astype(jnp.float32)
    grad_scores = jnp.einsum(
        "thd,jhd->htj", grad_blk, value_blk, preferred_element_type=jnp.float32
    )
    score_grad = (grad_scores * decay_mask).astype(jnp.bfloat16)
    grad_q = jnp.einsum(
        "htj,jhd->thd", score_grad, key_blk, preferred_element_type=jnp.float32
    ) + rise * jnp.einsum("the,hde->thd", broad_derivative_matrix, kv_state, precision=exact_mode)
    grad_k = jnp.einsum(
        "htj,thd->jhd", score_grad, query_blk, preferred_element_type=jnp.float32
    ) + tail_weight * jnp.einsum(
        "the,hde->thd", value_blk.astype(jnp.float32), grad_state, precision=exact_mode
    )
    grad_v = jnp.einsum(
        "htj,thd->jhd", attn_probs, grad_blk, preferred_element_type=jnp.float32
    ) + tail_weight * jnp.einsum(
        "thd,hde->the", key_blk.astype(jnp.float32), grad_state, precision=exact_mode
    )
    prior = jnp.exp(block_total)[:, None, None] * grad_state + jnp.einsum(
        "thd,the->hde",
        query_blk.astype(jnp.float32) * rise,
        broad_derivative_matrix,
        precision=exact_mode,
    )
    return (prior, (grad_q, grad_k, grad_v))


def combine(earlier, later):
    return (earlier[0] + later[0], jnp.exp(later[0])[:, None, None] * earlier[1] + later[1])


def per_device(
    query_rows,
    key_rows,
    value_rows,
    gate_logits,
    log_decay,
    norm_gain,
    state_in,
    cotangent,
    regroup,
):
    tok_rows = query_rows.shape[0]
    width_local = query_rows.shape[1]
    heads_here = state_in.shape[0]
    head_size = state_in.shape[1]
    blocks = tok_rows // BLOCK

    def divided_segments(array):
        return array.reshape((blocks, BLOCK, heads_here, head_size))

    query_b = divided_segments(query_rows)
    key_b = divided_segments(key_rows)
    value_b = divided_segments(value_rows)
    decay_b = log_decay.reshape((blocks, BLOCK, heads_here))
    zero_state = jnp.zeros((heads_here, head_size, head_size), jnp.float32)
    forward = lax.scan(block_forward, zero_state, (query_b, key_b, value_b, decay_b))
    local_end = forward[0]
    local_out, attn_probs, decay_mask, cum_log, local_starts = forward[1]
    dev_log = jnp.cumsum(log_decay, axis=0)
    dev_total = dev_log[-1]
    prefix_log, prefix_state = carried_in(
        (dev_total, local_end), "ctx", combine, (jnp.zeros_like(dev_total), zero_state), False
    )
    state_start = jnp.exp(prefix_log)[:, None, None] * state_in + prefix_state
    query_view = query_rows.reshape((tok_rows, heads_here, head_size))
    attended = local_out.reshape((tok_rows, heads_here, head_size)) + jnp.exp(dev_log)[
        :, :, None
    ] * jnp.einsum(
        "thd,hde->the", query_view.astype(jnp.float32), state_start, precision=exact_mode
    )
    block_ends = dev_log.reshape((blocks, BLOCK, heads_here))[:, -1]
    offsets = jnp.concatenate([jnp.zeros((1, heads_here), jnp.float32), block_ends[:-1]], axis=0)
    true_starts = local_starts + jnp.exp(offsets)[:, :, None, None] * state_start[None]
    flat = attended.reshape((tok_rows, width_local))
    width_all = width_local * lax.axis_size("head")
    gate_on = jax.nn.sigmoid(gate_logits.astype(jnp.float32))
    broad_derivative_matrix = cotangent.astype(jnp.float32)
    scaled_grad = broad_derivative_matrix * gate_on * norm_gain[None, :]
    own_squares = jnp.sum(flat * flat, axis=1)
    sum_squares = lax.psum(own_squares, "head")
    inv_rms = lax.rsqrt(sum_squares / width_all + 1e-06)
    unit_rows = flat * inv_rms[:, None]
    cross_unit = lax.psum(jnp.sum(scaled_grad * unit_rows, axis=1), "head")
    grad_flat = inv_rms[:, None] * (scaled_grad - unit_rows * (cross_unit / width_all)[:, None])
    normed = flat * inv_rms[:, None] * norm_gain[None, :]
    gated = (normed * gate_on).astype(jnp.bfloat16)
    grad_gate = (broad_derivative_matrix * normed * gate_on * (1.0 - gate_on)).astype(jnp.bfloat16)
    grad_attended = grad_flat.astype(jnp.bfloat16)
    peers = lax.axis_size("ctx")
    ctx_place = lax.axis_index("ctx")
    pieces = gated.reshape((peers, tok_rows // peers, width_local))
    table = regroup.reshape((peers, peers))
    wanted = ctx_place * peers + jnp.arange(peers)
    send_pick = jnp.sum(
        (table[:, :, None] == wanted[None, None, :]).astype(jnp.int32), axis=1
    ).astype(jnp.bfloat16)
    outgoing = jnp.einsum(
        "dl,lrw->drw", send_pick, pieces, preferred_element_type=jnp.float32
    ).astype(jnp.bfloat16)
    arrived = lax.all_to_all(outgoing, "ctx", split_axis=0, concat_axis=0, tiled=True)
    my_list = lax.dynamic_index_in_dim(table, ctx_place, 0, keepdims=False)
    take_pick = ((my_list // peers)[:, None] == jnp.arange(peers)[None, :]).astype(jnp.bfloat16)
    gated_out = (
        jnp.einsum("sj,jrw->srw", take_pick, arrived, preferred_element_type=jnp.float32)
        .astype(jnp.bfloat16)
        .reshape((tok_rows, width_local))
    )
    backward = lax.scan(
        block_backward,
        zero_state,
        (
            query_b,
            key_b,
            value_b,
            divided_segments(grad_attended),
            attn_probs,
            decay_mask,
            cum_log,
            true_starts,
        ),
        reverse=True,
    )
    local_grad_start = backward[0]
    grad_q, grad_k, grad_v = backward[1]
    carried_back = carried_in(
        (dev_total, local_grad_start), "ctx", combine, (jnp.zeros_like(dev_total), zero_state), True
    )
    grad_after = carried_back[1]
    tail_dev = jnp.exp(dev_total[None, :] - dev_log)[:, :, None]
    key_view = key_rows.reshape((tok_rows, heads_here, head_size)).astype(jnp.float32)
    value_view = value_rows.reshape((tok_rows, heads_here, head_size)).astype(jnp.float32)
    grad_key = grad_k.reshape((tok_rows, heads_here, head_size)) + tail_dev * jnp.einsum(
        "the,hde->thd", value_view, grad_after, precision=exact_mode
    )
    grad_value = grad_v.reshape((tok_rows, heads_here, head_size)) + tail_dev * jnp.einsum(
        "thd,hde->the", key_view, grad_after, precision=exact_mode
    )
    grad_query = grad_q.reshape((tok_rows, width_local)).astype(jnp.bfloat16)
    grad_key = grad_key.reshape((tok_rows, width_local)).astype(jnp.bfloat16)
    grad_value = grad_value.reshape((tok_rows, width_local)).astype(jnp.bfloat16)
    return (gated_out, grad_query, grad_key, grad_value, grad_gate)


def solution(mesh):
    in_specs = (
        P("ctx", "head"),
        P("ctx", "head"),
        P("ctx", "head"),
        P("ctx", "head"),
        P("ctx", "head"),
        P("head"),
        P("head", None, None),
        P("ctx", "head"),
        P(),
    )
    out_specs = (
        P("ctx", "head"),
        P("ctx", "head"),
        P("ctx", "head"),
        P("ctx", "head"),
        P("ctx", "head"),
    )
    return jax.shard_map(
        per_device, mesh=mesh, in_specs=in_specs, out_specs=out_specs, check_vma=False
    )
```

profile of v0, /device:TPU:0, one launch (start us, length us, event | category | flops | bytes accessed | tf_op | source)
XLA Modules:
  0.0 115.3 jit_solution(3352040745296947182)
XLA Ops:
  0.7 1.0 reduce-window.12
  4.7 1.2 %dynamic-slice.5 = u32[1]{0:T(128)} dynamic-slice(u32[32]{0:T(128)} %constant.144, u32[]{:T(128)S(6)} %add.141), dynamic_slice_sizes={1} | dynamic-slice | bytes 12
  6.0 0.8 dynamic-update-slice
  6.8 1.7 %fusion.21 = bf16[128,128]{1,0:T(8,128)(2,1)S(1)} fusion(bf16[1024,128]{1,0:T(8,128)(2,1)S(1)} %copy-done, bf16[1024,128]{1,0:T(8,128)(2,1)} %param.14, f32[1024]{0:T(1024)S(1)} %get-tuple-element.264, f32[]{:T(128)} %bitcast.21), kind=kOutput, calls=%fused_computation.44 | convolution fusion | flops 201621504 | bytes 561156 | tf_op jit(solution)/shard_map/while/body/eval_jaxpr/thd,the->hde/dot_general | solution.py:52
  8.5 15.9 %all-gather = bf16[1024,128]{1,0:T(8,128)(2,1)S(1)} all-gather(bf16[128,128]{1,0:T(8,128)(2,1)S(1)} %fusion.21), channel_id=2, replica_groups=mesh['ctx'=8,'head'=4] {'ctx'}, dimensions={0}, use_global_device_ids=true | all-gather | bytes 294912 | tf_op jit(solution)/shard_map/all_gather | solution.py:17
  24.3 16.9 %all-reduce = bf16[8]{0:T(256)(128)(2,1)S(1)} all-reduce(bf16[8]{0:T(256)(128)(2,1)S(1)} %dynamic-update-slice), channel_id=1, replica_groups=mesh['ctx'=8,'head'=4] {'ctx'}, use_global_device_ids=true, to_apply=%add | all-reduce | flops 8 | bytes 32
  41.4 0.7 multiply_convert_fusion.1
  42.2 0.7 convolution_bitcast_fusion.10
  43.8 9.9 %psum.14 = f32[1024]{0:T(1024)S(1)} all-reduce(f32[1024]{0:T(1024)S(1)} %get-tuple-element.269), channel_id=1, replica_groups=mesh['ctx'=8,'head'=4] {'head'}, use_global_device_ids=true, to_apply=%region_6.7 | all-reduce | flops 1024 | bytes 8192 | tf_op jit(solution)/shard_map/psum | solution.py:147
  53.7 1.4 %multiply_reduce_fusion = f32[1024]{0:T(1024)S(1)} fusion(f32[1024,128]{1,0:T(8,128)S(1)} %get-tuple-element.270, bf16[1024,128]{1,0:T(8,128)(2,1)} %param.20, f32[128]{0:T(128)} %param.18, f32[1024]{0:T(1024)S(1)} %add_rsqrt_fusion, bf16[1024,128]{1,0:T(8,128)(2,1)} %param.16), kind=kLoop, calls=%fused_computation.55 | loop fusion | flops 1309696 | bytes 1057280 | tf_op jit(solution)/shard_map/reduce_sum | solution.py:150
  55.1 8.5 %psum.15 = f32[1024]{0:T(1024)} all-reduce(f32[1024]{0:T(1024)S(1)} %multiply_reduce_fusion), channel_id=1, replica_groups=mesh['ctx'=8,'head'=4] {'head'}, use_global_device_ids=true, to_apply=%region_8.9 | all-reduce | flops 1024 | bytes 8192 | tf_op jit(solution)/shard_map/psum | solution.py:150
  63.7 0.7 broadcast_multiply_fusion
  64.4 2.3 %fusion.26 = (bf16[1024,128]{1,0:T(8,128)(2,1)}, bf16[1024,128]{1,0:T(8,128)(2,1)}, bf16[1024,128]{1,0:T(8,128)(2,1)}) fusion(bf16[1024,128]{1,0:T(8,128)(2,1)} %param.20, f32[1024,128]{1,0:T(8,128)S(1)} %get-tuple-element.270, f32[128]{0:T(128)} %param.18, f32[1024]{0:T(1024)S(1)} %add_rsqrt_fusion, bf16[1024,128]{1,0:T(8,128)(2,1)} %param.16, ...), kind=kLoop, calls=%fused_computation.51 | loop fusion | flops 2621440 | bytes 1843712 | tf_op jit(solution)/shard_map/convert_element_type | solution.py:154
  66.7 0.7 reshape.467
  67.5 1.2 %convolution_convert_fusion.1 = bf16[8,128,128]{2,0,1:T(8,128)(2,1)S(1)} fusion(bf16[8,128,128]{2,1,0:T(8,128)(2,1)} %bitcast.177, s32[8,8]{1,0:T(8,128)S(1)} %convert_reduce_fusion), kind=kOutput, calls=%fused_computation.38 | convolution fusion | flops 2228288 | bytes 524544 | tf_op jit(solution)/shard_map/dl,lrw->drw/dot_general | solution.py:164
  68.8 0.7 copy.53
  69.5 11.3 %all-to-all-start = ((bf16[8,128,128]{2,1,0:T(8,128)(2,1)}), bf16[8,128,128]{2,1,0:T(8,128)(2,1)S(1)}, u32[]{:S(2)}, u32[]{:S(2)}) async-start(bf16[8,128,128]{2,1,0:T(8,128)(2,1)} %copy.53), calls=%async_computation | async-start | bytes 524288 | tf_op jit(solution)/shard_map/all_to_all | solution.py:167
  80.8 2.7 %convolution_bitcast_fusion.2 = f32[1,128,1024]{1,2,0:T(8,128)} fusion(bf16[1024,128]{1,0:T(8,128)(2,1)} %get-tuple-element.267, bf16[1024,1024]{1,0:T(8,128)(2,1)S(1)} %multiply_convert_fusion.1), kind=kOutput, calls=%fused_computation.10 | convolution fusion | flops 268435456 | bytes 2883584 | tf_op jit(solution)/shard_map/while/body/eval_jaxpr/htj,thd->jhd/dot_general | solution.py:80
  83.5 0.7 fusion.22
  84.2 0.7 multiply_convert_fusion
  85.0 0.7 convolution_bitcast_fusion.5
  85.7 0.7 convolution_bitcast_fusion.7
  86.4 14.9 %all-gather.1 = bf16[1024,128]{1,0:T(8,128)(2,1)S(1)} all-gather(bf16[128,128]{1,0:T(8,128)(2,1)S(1)} %fusion.22), channel_id=3, replica_groups=mesh['ctx'=8,'head'=4] {'ctx'}, dimensions={0}, use_global_device_ids=true | all-gather | bytes 294912 | tf_op jit(solution)/shard_map/all_gather | solution.py:17
  101.3 9.0 %while.8 = (s32[]{:T(128)}, f32[1,128,128]{2,1,0:T(8,128)S(1)}, s32[]{:T(128)}, bf16[8,1]{0,1:T(2,128)(2,1)S(1)}, bf16[8,1,128,128]{3,2,1,0:T(8,128)(2,1)S(1)}, ...) while((s32[]{:T(128)}, f32[1,128,128]{2,1,0:T(8,128)S(1)}, s32[]{:T(128)}, bf16[8,1]{0,1:T(2,128)(2,1)S(1)}, ...), condition=%wide.region_10.11_spmd, body=%wide.region_9.10_spmd.sunk | while | flops 49158 | bytes 163997 | solution.py:32
  103.2 0.7 convert_add_fusion.5
  104.5 0.7 convert_add_fusion.5
  105.8 0.7 convert_add_fusion.5
  107.1 0.7 convert_add_fusion.5
  110.7 1.1 fusion.18
  111.8 1.1 fusion.20
  113.2 1.1 fusion.19
  114.6 0.7 copy.55
  (52 shorter events, 10.0 us)
Async XLA Ops:
  0.6 6.1 %copy-start = (bf16[1024,128]{1,0:T(8,128)(2,1)S(1)}, bf16[1024,128]{1,0:T(8,128)(2,1)}, u32[]{:S(2)}) copy-start(bf16[1024,128]{1,0:T(8,128)(2,1)} %param.15) | copy-start | bytes 786436
  0.6 40.7 %copy-start.2 = (bf16[1024,128]{1,0:T(8,128)(2,1)S(1)}, bf16[1024,128]{1,0:T(8,128)(2,1)}, u32[]{:S(2)}) copy-start(bf16[1024,128]{1,0:T(8,128)(2,1)} %param.14) | copy-start | bytes 786436
  0.7 40.7 %copy-start.1 = (bf16[1024,128]{1,0:T(8,128)(2,1)S(1)}, bf16[1024,128]{1,0:T(8,128)(2,1)}, u32[]{:S(2)}) copy-start(bf16[1024,128]{1,0:T(8,128)(2,1)} %param.13) | copy-start | bytes 786436
  4.7 37.4 %copy-start.6 = (f32[1024]{0:T(1024)}, f32[1024]{0:T(1024)S(1)}, u32[]{:S(2)}) copy-start(f32[1024]{0:T(1024)S(1)} %get-tuple-element.265) | copy-start | bytes 12292
  41.3 0.8 copy-start.8
  42.1 0.8 copy-start.5
  68.7 14.7 %copy-start.3 = (bf16[1024,128]{1,0:T(8,128)(2,1)S(1)}, bf16[1024,128]{1,0:T(8,128)(2,1)}, u32[]{:S(2)}) copy-start(bf16[1024,128]{1,0:T(8,128)(2,1)} %get-tuple-element.267) | copy-start | bytes 786436
  69.5 14.7 %copy-start.7 = (f32[1024]{0:T(1024)S(1)}, f32[1024]{0:T(1024)}, u32[]{:S(2)}) copy-start(f32[1024]{0:T(1024)} %copy-done.6) | copy-start | bytes 12292
  69.5 44.8 %all-to-all-start = ((bf16[8,128,128]{2,1,0:T(8,128)(2,1)}), bf16[8,128,128]{2,1,0:T(8,128)(2,1)S(1)}, u32[]{:S(2)}, u32[]{:S(2)}) async-start(bf16[8,128,128]{2,1,0:T(8,128)(2,1)} %copy.53), calls=%async_computation | async-start | bytes 524288 | tf_op jit(solution)/shard_map/all_to_all | solution.py:167
  85.7 15.6 %copy-start.9 = (bf16[8,1]{0,1:T(2,128)(2,1)S(1)}, bf16[8,1]{0,1:T(2,128)(2,1)}, u32[]{:S(2)}) copy-start(bf16[8,1]{0,1:T(2,128)(2,1)} %copy-done.8) | copy-start | bytes 52
  86.4 25.3 %copy-start.4 = (f32[1,128,1024]{1,2,0:T(8,128)S(1)}, f32[1,128,1024]{1,2,0:T(8,128)}, u32[]{:S(2)}) copy-start(f32[1,128,1024]{1,2,0:T(8,128)} %convolution_bitcast_fusion.2) | copy-start | bytes 1572868
where the time goes:
time: 116 us; the launch traced here: 115 us
  blocking collectives  66.2 us (57%)
  matrix products  15 us (13%)
  starting transfers between devices  11.3 us (10%)
  other arithmetic  10.4 us (9%)
  local copies, waits for them, and re-layouts  9.99 us (9%)
  between operations  2.25 us (2%)
    all_gather x2, blocking collectives, carried_in(): lax.all_gather(a.astype(kind), axis)  30.8 us
    unnamed x1, blocking collectives  16.9 us
    all_to_all x1, starting transfers between devices, per_device(): lax.all_to_all(outgoing, 'ctx', split_axis=0, concat_axis=0, tiled=True)  11.3 us
    psum x1, blocking collectives, per_device(): sum_squares = lax.psum(own_squares, 'head')  9.92 us
    psum x1, blocking collectives, per_device(): cross_unit = lax.psum(jnp.sum(scaled_grad * unit_rows, axis=1), 'head')  8.55 us
    add x7, other arithmetic, combine(): jnp.exp(later[0])[:, None, None] * earlier[1] + later[1]  4.59 us
    exp x7, local copies, waits for them, and re-layouts, combine(): jnp.exp(later[0])[:, None, None] * earlier[1] + later[1]  4.14 us
    dot_general x1, matrix products, block_backward(): jnp.einsum('htj,thd->jhd', attn_probs, grad_blk, preferred_element_type=j...  2.67 us
  transfers between devices with their start and end apart: 1, of which 0 were waited for; matrix products, arithmetic and copies ran while one was open for 16% of the time, Pallas kernels for 0%

commit v1 on v0

v1 whole, which is shorter than its diff:
```python
import functools

import jax
import jax.numpy as jnp
from jax import lax
from jax.experimental import pallas as pl
from jax.experimental.pallas import tpu as pltpu
from jax.sharding import PartitionSpec as P

F32 = jnp.float32
BF16 = jnp.bfloat16
MESH = pl.DeviceIdType.MESH
T = 128
NT = (((1,), (1,)), ((), ()))
NN = (((1,), (0,)), ((), ()))
TN = (((0,), (0,)), ((), ()))


def dot(a, b, dims):
    return lax.dot_general(a, b, dims, preferred_element_type=F32)


def kernel(
    n, m, rows,
    q_hbm, k_hbm, v_hbm, gate_hbm, ct_hbm, decay_ref, gain_ref, state_ref, regroup,
    go_out, gq_out, gk_out, gv_out, gg_out,
    q, k, v, gate, ct,
    cum_b, rise_b, tail_b, mask, probs, att, scaled, gated, grad, qr, gk_acc, gv_acc,
    go, gq, gk, gv, gg,
    tots, swap_out, swap_in, f_out, f_in, b_out, b_in, stat, a_out, a_in, start_state,
    in_sem, out_sem, tot_send, tot_recv, swap_send, swap_recv,
    f_send, f_recv, b_send, b_recv, h_send, h_recv, a_send, a_recv,
):
    me = lax.axis_index("ctx")
    head = lax.axis_index("head")
    chip = me // 2
    core = me % 2
    mate = me + 1 - 2 * core
    chips = n // 2
    nb = rows // T
    piece = rows // n
    width_all = m * T
    shift = n.bit_length() - 1

    loads = [
        pltpu.make_async_copy(src, dst, in_sem.at[i])
        for i, (src, dst) in enumerate(
            [(k_hbm, k), (v_hbm, v), (q_hbm, q), (gate_hbm, gate), (ct_hbm, ct)]
        )
    ]
    for load in loads:
        load.start()

    barrier = pltpu.get_barrier_semaphore()

    def greet_ctx(o, c):
        pl.semaphore_signal(
            barrier, inc=1, device_id={"ctx": lax.rem(me + o, n)}, device_id_type=MESH
        )
        return c

    def greet_head(o, c):
        pl.semaphore_signal(
            barrier, inc=1, device_id={"head": lax.rem(head + o, m)}, device_id_type=MESH
        )
        return c

    lax.fori_loop(1, n, greet_ctx, 0)
    lax.fori_loop(1, m, greet_head, 0)

    row_i = lax.broadcasted_iota(jnp.int32, (T, T), 0)
    col_i = lax.broadcasted_iota(jnp.int32, (T, T), 1)
    upper = (row_i <= col_i).astype(F32)
    partial_sums = lax.dot_general(
        decay_ref[...], upper, NN, precision=lax.Precision.HIGHEST, preferred_element_type=F32
    )
    crow = []
    offset = jnp.zeros((1, 1), F32)
    for r in range(nb):
        row = partial_sums[r : r + 1, :]
        crow.append(row + offset)
        offset = offset + row[:, T - 1 : T]
    total = jnp.broadcast_to(crow[-1][:, T - 1 : T], (1, T))
    tots[pl.ds(me, 1)] = jnp.broadcast_to(total, (8, T))[None]
    for r in range(nb):
        sl = slice(r * T, (r + 1) * T)
        cb = jnp.transpose(jnp.broadcast_to(crow[r], (T, T)))
        cum_b[sl, :] = cb
        rise_b[sl, :] = jnp.exp(cb)
        tail_b[sl, :] = jnp.exp(total - cb)

    loads[0].wait()
    loads[1].wait()
    weighted = (k[...].astype(F32) * tail_b[...]).astype(BF16)
    local = dot(weighted, v[...], TN)
    swap_out[0] = local

    pl.semaphore_wait(barrier, n - 1 + m - 1)

    def swap_copy(i):
        return pltpu.make_async_remote_copy(
            src_ref=swap_out.at[i], dst_ref=swap_in.at[i],
            send_sem=swap_send.at[i], recv_sem=swap_recv.at[i],
            device_id={"ctx": mate}, device_id_type=MESH,
        )

    swap_copy(0).start()

    def tot_copy(slot, to):
        return pltpu.make_async_remote_copy(
            src_ref=tots.at[me], dst_ref=tots.at[slot],
            send_sem=tot_send.at[to], recv_sem=tot_recv.at[slot],
            device_id={"ctx": to}, device_id_type=MESH,
        )

    def tot_go(o, c):
        tot_copy(me, lax.rem(me + o, n)).start()
        return c

    lax.fori_loop(1, n, tot_go, 0)

    loads[2].wait()
    causal = row_i >= col_i

    def decay_tile(a, b):
        diff = cum_b[a * T : (a + 1) * T, :] - crow[b]
        if a == b:
            return jnp.where(causal, jnp.exp(jnp.where(causal, diff, 0.0)), 0.0)
        return jnp.exp(diff)

    def scores_for(a):
        w = (a + 1) * T
        s = dot(q[a * T : w, :], k[:w, :], NT)
        for b in range(a + 1):
            d = decay_tile(a, b)
            mask[a * T : w, b * T : (b + 1) * T] = d
            probs[a * T : w, b * T : (b + 1) * T] = (s[:, b * T : (b + 1) * T] * d).astype(BF16)

    half = nb // 4
    for a in range(half):
        scores_for(a)

    def tot_wait(o, c):
        tot_copy(lax.rem(me + o, n), lax.rem(me + o, n)).wait_recv()
        return c

    lax.fori_loop(1, n, tot_wait, 0)
    swap_copy(0).wait_recv()

    def tot_row(i):
        return tots[pl.ds(i, 1)][0, 0:1, :]

    mine, other = swap_out[0], swap_in[0]
    is_late = core == 1
    later = jnp.exp(jnp.where(is_late, total, tot_row(mate)))
    f_out[...] = (later * jnp.where(is_late, other, mine) + jnp.where(is_late, mine, other)).astype(BF16)

    def f_copy(slot, to):
        return pltpu.make_async_remote_copy(
            src_ref=f_out, dst_ref=f_in.at[slot],
            send_sem=f_send.at[to], recv_sem=f_recv.at[slot],
            device_id={"ctx": 2 * to + core}, device_id_type=MESH,
        )

    def f_go(to, c):
        f_copy(chip, to).start()
        return c

    lax.fori_loop(chip + 1, chips, f_go, 0)

    for a in range(half, nb):
        scores_for(a)
    for a in range(nb):
        w = (a + 1) * T
        att[a * T : w, :] = dot(probs[a * T : w, :w], v[:w, :], NN)
    qr[...] = (q[...].astype(F32) * rise_b[...]).astype(BF16)
    loads[3].wait()
    loads[4].wait()
    on = jax.nn.sigmoid(gate[...].astype(F32))
    scaled[...] = ct[...].astype(F32) * on * gain_ref[...]

    def chip_total(i):
        return tot_row(2 * i) + tot_row(2 * i + 1)

    def f_join(i, state):
        f_copy(i, i).wait_recv()
        return jnp.exp(chip_total(i)) * state + f_in[pl.ds(i, 1)][0].astype(F32)

    state = lax.fori_loop(0, chip, f_join, state_ref[0])
    state = jnp.where(is_late, jnp.exp(tot_row(mate)) * state + other, state)
    start_state[...] = state.astype(BF16)

    for r in range(nb):
        sl = slice(r * T, (r + 1) * T)
        flat = att[sl, :] + rise_b[sl, :] * dot(q[sl, :], start_state[...], NN)
        att[sl, :] = flat
        stat[pl.ds(head, 1), r : r + 1, :] = jnp.sum(
            jnp.transpose(flat * flat), axis=0, keepdims=True
        )[None]
        stat[pl.ds(head, 1), nb + r : nb + r + 1, :] = jnp.sum(
            jnp.transpose(flat * scaled[sl, :]), axis=0, keepdims=True
        )[None]

    def h_copy(slot, to):
        return pltpu.make_async_remote_copy(
            src_ref=stat.at[head], dst_ref=stat.at[slot],
            send_sem=h_send.at[to], recv_sem=h_recv.at[slot],
            device_id={"head": to}, device_id_type=MESH,
        )

    def h_go(o, c):
        h_copy(head, lax.rem(head + o, m)).start()
        return c

    lax.fori_loop(1, m, h_go, 0)

    def h_join(o, acc):
        i = lax.rem(head + o, m)
        h_copy(i, i).wait_recv()
        return acc + stat[pl.ds(i, 1)][0]

    sums = lax.fori_loop(1, m, h_join, stat[pl.ds(head, 1)][0])
    inv = lax.rsqrt(sums[:nb] / width_all + 1e-06)
    coef = inv * inv * inv * sums[nb:] / width_all
    for r in range(nb):
        sl = slice(r * T, (r + 1) * T)
        inv_b = jnp.transpose(jnp.broadcast_to(inv[r : r + 1, :], (T, T)))
        coef_b = jnp.transpose(jnp.broadcast_to(coef[r : r + 1, :], (T, T)))
        flat = att[sl, :]
        grad[sl, :] = (inv_b * scaled[sl, :] - flat * coef_b).astype(BF16)
        att[sl, :] = flat * inv_b * gain_ref[...]

    back = dot(qr[...], grad[...], TN)
    swap_out[1] = back
    swap_copy(1).start()

    for r in range(nb):
        sl = slice(r * T, (r + 1) * T)
        on = jax.nn.sigmoid(gate[sl, :].astype(F32))
        normed = att[sl, :]
        out = (normed * on).astype(BF16)
        for part in range(T // piece):
            gated[r * (T // piece) + part] = out[part * piece : (part + 1) * piece]
        gg[sl, :] = (ct[sl, :].astype(F32) * normed * on * (1.0 - on)).astype(BF16)

    swap_copy(1).wait_recv()
    mine_b, other_b = swap_out[1], swap_in[1]
    earlier = jnp.exp(jnp.where(is_late, tot_row(mate), total))
    b_out[...] = (
        earlier * jnp.where(is_late, mine_b, other_b) + jnp.where(is_late, other_b, mine_b)
    ).astype(BF16)

    def b_copy(slot, to):
        return pltpu.make_async_remote_copy(
            src_ref=b_out, dst_ref=b_in.at[slot],
            send_sem=b_send.at[to], recv_sem=b_recv.at[slot],
            device_id={"ctx": 2 * to + core}, device_id_type=MESH,
        )

    def b_go(to, c):
        b_copy(chip, to).start()
        return c

    lax.fori_loop(0, chip, b_go, 0)

    def pick(d):
        def one(s, found):
            p = regroup[d * n + s]
            apart = lax.shift_right_logical(p, shift) - me
            return found + (1 - jnp.minimum(apart * apart, 1)) * (p & (n - 1))

        return lax.fori_loop(0, n, one, jnp.int32(0), unroll=8)

    def wanted(d):
        return gated[pick(d)]

    def a_copy(slot, to):
        return pltpu.make_async_remote_copy(
            src_ref=a_out.at[to], dst_ref=a_in.at[slot],
            send_sem=a_send.at[to], recv_sem=a_recv.at[slot],
            device_id={"ctx": to}, device_id_type=MESH,
        )

    def a_go(o, c):
        to = lax.rem(me + o, n)
        a_out[to] = wanted(to)
        a_copy(me, to).start()
        return c

    lax.fori_loop(1, n, a_go, 0)
    a_in[me] = wanted(me)

    stores = [
        pltpu.make_async_copy(src, dst, out_sem.at[i])
        for i, (src, dst) in enumerate(
            [(go, go_out), (gq, gq_out), (gk, gk_out), (gv, gv_out), (gg, gg_out)]
        )
    ]
    stores[4].start()

    for a in range(nb):
        w = (a + 1) * T
        sl = slice(a * T, w)
        ds = (dot(grad[sl, :], v[:w, :], NT) * mask[sl, :w]).astype(BF16)
        gq[sl, :] = (
            dot(ds, k[:w, :], NN) + rise_b[sl, :] * dot(grad[sl, :], start_state[...], NT)
        ).astype(BF16)
        dk = dot(ds, q[sl, :], TN)
        dv = dot(probs[sl, :w], grad[sl, :], TN)
        if a:
            gk_acc[: a * T, :] += dk[: a * T]
            gv_acc[: a * T, :] += dv[: a * T]
        gk_acc[sl, :] = dk[a * T :]
        gv_acc[sl, :] = dv[a * T :]
    stores[1].start()

    def b_join(o, state):
        i = chips - 1 - o
        b_copy(i, i).wait_recv()
        return jnp.exp(chip_total(i)) * state + b_in[pl.ds(i, 1)][0].astype(F32)

    after = lax.fori_loop(0, chips - 1 - chip, b_join, jnp.zeros((T, T), F32))
    after = jnp.where(is_late, after, jnp.exp(tot_row(mate)) * after + other_b).astype(BF16)
    gk[...] = (gk_acc[...] + tail_b[...] * dot(v[...], after, NT)).astype(BF16)
    stores[2].start()
    gv[...] = (gv_acc[...] + tail_b[...] * dot(k[...], after, NN)).astype(BF16)
    stores[3].start()

    def a_wait(o, c):
        i = lax.rem(me + o, n)
        a_copy(i, i).wait_recv()
        return c

    lax.fori_loop(1, n, a_wait, 0)
    for s in range(n):
        src = lax.shift_right_logical(regroup[me * n + s], shift)
        go[s * piece : (s + 1) * piece, :] = a_in[src]
    stores[0].start()

    swap_copy(0).wait_send()
    swap_copy(1).wait_send()

    def end_ctx(o, c):
        to = lax.rem(me + o, n)
        tot_copy(to, to).wait_send()
        a_copy(to, to).wait_send()
        return c

    lax.fori_loop(1, n, end_ctx, 0)

    def end_head(o, c):
        to = lax.rem(head + o, m)
        h_copy(to, to).wait_send()
        return c

    lax.fori_loop(1, m, end_head, 0)

    def end_f(to, c):
        f_copy(to, to).wait_send()
        return c

    lax.fori_loop(chip + 1, chips, end_f, 0)

    def end_b(to, c):
        b_copy(to, to).wait_send()
        return c

    lax.fori_loop(0, chip, end_b, 0)
    for store in stores:
        store.wait()


def per_device(n, m, query, key, value, gate, decay, gain, state_in, cotangent, regroup):
    rows = query.shape[0]
    chips = n // 2
    nb = rows // T
    piece = rows // n
    big = lambda kind: pltpu.VMEM((rows, T), kind)
    dma = pltpu.SemaphoreType.DMA
    hbm = pl.BlockSpec(memory_space=pl.ANY)
    vmem = pl.BlockSpec(memory_space=pltpu.VMEM)
    smem = pl.BlockSpec(memory_space=pltpu.SMEM)
    return pl.pallas_call(
        functools.partial(kernel, n, m, rows),
        out_shape=[jax.ShapeDtypeStruct((rows, T), BF16)] * 5,
        in_specs=[hbm] * 5 + [vmem] * 3 + [smem],
        out_specs=[hbm] * 5,
        scratch_shapes=[big(BF16)] * 5
        + [big(F32)] * 3
        + [
            pltpu.VMEM((rows, rows), F32),
            pltpu.VMEM((rows, rows), BF16),
            big(F32), big(F32), pltpu.VMEM((n, piece, T), BF16), big(BF16), big(BF16), big(F32), big(F32),
        ]
        + [big(BF16)] * 5
        + [
            pltpu.VMEM((n, 8, T), F32),
            pltpu.VMEM((2, T, T), F32),
            pltpu.VMEM((2, T, T), F32),
            pltpu.VMEM((T, T), BF16),
            pltpu.VMEM((chips, T, T), BF16),
            pltpu.VMEM((T, T), BF16),
            pltpu.VMEM((chips, T, T), BF16),
            pltpu.VMEM((m, 2 * nb, T), F32),
            pltpu.VMEM((n, piece, T), BF16),
            pltpu.VMEM((n, piece, T), BF16),
            pltpu.VMEM((T, T), BF16),
        ]
        + [
            dma((5,)), dma((5,)), dma((n,)), dma((n,)), dma((2,)), dma((2,)),
            dma((chips,)), dma((chips,)), dma((chips,)), dma((chips,)),
            dma((m,)), dma((m,)), dma((n,)), dma((n,)),
        ],
        compiler_params=pltpu.CompilerParams(
            collective_id=0, has_side_effects=True, vmem_limit_bytes=62 << 20
        ),
        name="layer",
    )(
        query, key, value, gate, cotangent,
        decay.reshape((nb, T)), gain.reshape((1, T)), state_in, regroup,
    )


def solution(mesh):
    rows = P("ctx", "head")
    in_specs = (rows, rows, rows, rows, rows, P("head"), P("head", None, None), rows, P())
    body = functools.partial(per_device, mesh.shape["ctx"], mesh.shape["head"])
    return jax.shard_map(
        body, mesh=mesh, in_specs=in_specs, out_specs=(rows,) * 5, check_vma=False
    )
```

time: 116 us -> 36.1 us (0.31)
  blocking collectives: 66.2 us -> 0 us
  Pallas kernels: 0 us -> 29.5 us
  matrix products: 15 us -> 0 us
  starting transfers between devices: 11.3 us -> 0 us
  other arithmetic: 10.4 us -> 0 us
  local copies, waits for them, and re-layouts: 9.99 us -> 5.55 us
  between operations: 2.25 us -> 0.66 us
    all_gather x2 -> x0, blocking collectives: 30.8 us -> none  [carried_in(): lax.all_gather(a.astype(kind), axis)]
    pallas_call x0 -> x1, Pallas kernels: none -> 29.5 us  [per_device(): pl.pallas_call(functools.partial(kernel, n, m, rows), out_shape=[jax.Shap...]
    psum x2 -> x0, blocking collectives: 18.5 us -> none  [the longest x1 9.92 us: per_device(): sum_squares = lax.psum(own_squares, 'head')]
    unnamed x1 -> x0, blocking collectives: 16.9 us -> none
    dot_general x17 -> x0, matrix products: 15 us -> none  [the longest x1 2.67 us: block_backward(): jnp.einsum('htj,thd->jhd', attn_probs, grad_blk, preferred_element_type=j...]
    all_to_all x1 -> x0, starting transfers between devices: 11.3 us -> none  [per_device(): lax.all_to_all(outgoing, 'ctx', split_axis=0, concat_axis=0, tiled=True)]
    add x8 -> x0, other arithmetic: 4.6 us -> none  [the longest x7 4.59 us: combine(): jnp.exp(later[0])[:, None, None] * earlier[1] + later[1]]
    exp x8 -> x0, local copies, waits for them, and re-layouts: 4.15 us -> none  [the longest x7 4.14 us: combine(): jnp.exp(later[0])[:, None, None] * earlier[1] + later[1]]
  transfers between devices with their start and end apart: 1 -> 0, of which waited for: 0 -> 0; matrix products, arithmetic and copies ran while one was open for 16% -> 0% of each run, Pallas kernels for 0% -> 0%
where the time goes in v1:
time: 36.1 us; the launch traced here: 35.7 us
  Pallas kernels  29.5 us (82%)
  local copies, waits for them, and re-layouts  5.55 us (15%)
  between operations  0.66 us (2%)
    pallas_call x1, Pallas kernels, per_device(): pl.pallas_call(functools.partial(kernel, n, m, rows), out_shape=[jax.Shap...  29.5 us
    unnamed x13, local copies, waits for them, and re-layouts  5.55 us

profile of v1, /device:TPU:0, one launch (start us, length us, event | category | flops | bytes accessed | tf_op | source)
XLA Modules:
  0.0 35.7 jit_solution(8501714599113923804)
XLA Ops:
  0.6 29.5 %layer.1 = (bf16[1024,128]{1,0:T(8,128)(2,1)}, bf16[1024,128]{1,0:T(8,128)(2,1)}, bf16[1024,128]{1,0:T(8,128)(2,1)}, bf16[1024,128]{1,0:T(8,128)(2,1)}, bf16[1024,128]{1,0:T(8,128)(2,1)}) custom-call(bf16[1024,128]{1,0:T(8,128)(2,1)} %q_hbm.1, bf16[1024,128]{1,0:T(8,128)(2,1)} %k_hbm.1, bf16[1024,128]{1,0:T(8,128)(2,1)} %v_hbm.1, ...), custom_call_target="tpu_custom_call" | custom-call | tf_op jit(solution)/shard_map/layer/pallas_call | solution.py:383
  30.1 0.0 copy-start.3
  30.1 1.7 %copy.19 = bf16[1024,128]{1,0:T(8,128)(2,1)} copy(bf16[1024,128]{1,0:T(8,128)(2,1)} %get-tuple-element.10) | data formatting | bytes 524288
  31.8 0.0 copy-done.3
  31.8 0.0 copy-start.2
  31.9 0.7 %copy.20 = bf16[1024,128]{1,0:T(8,128)(2,1)} copy(bf16[1024,128]{1,0:T(8,128)(2,1)S(1)} %copy-done.3) | data formatting | bytes 524288
  32.6 0.3 copy-done.2
  32.9 0.0 copy-start.1
  32.9 0.7 %copy.21 = bf16[1024,128]{1,0:T(8,128)(2,1)} copy(bf16[1024,128]{1,0:T(8,128)(2,1)S(1)} %copy-done.2) | data formatting | bytes 524288
  33.6 0.3 copy-done.1
  33.9 0.0 copy-start
  33.9 0.7 %copy.22 = bf16[1024,128]{1,0:T(8,128)(2,1)} copy(bf16[1024,128]{1,0:T(8,128)(2,1)S(1)} %copy-done.1) | data formatting | bytes 524288
  34.6 0.3 copy-done
  35.0 0.7 %copy.23 = bf16[1024,128]{1,0:T(8,128)(2,1)} copy(bf16[1024,128]{1,0:T(8,128)(2,1)S(1)} %copy-done) | data formatting | bytes 524288
Async XLA Ops:
  30.1 1.7 %copy-start.3 = (bf16[1024,128]{1,0:T(8,128)(2,1)S(1)}, bf16[1024,128]{1,0:T(8,128)(2,1)}, u32[]{:S(2)}) copy-start(bf16[1024,128]{1,0:T(8,128)(2,1)} %get-tuple-element.11) | copy-start | bytes 786436
  31.8 1.0 %copy-start.2 = (bf16[1024,128]{1,0:T(8,128)(2,1)S(1)}, bf16[1024,128]{1,0:T(8,128)(2,1)}, u32[]{:S(2)}) copy-start(bf16[1024,128]{1,0:T(8,128)(2,1)} %get-tuple-element.12) | copy-start | bytes 786436
  32.9 1.0 %copy-start.1 = (bf16[1024,128]{1,0:T(8,128)(2,1)S(1)}, bf16[1024,128]{1,0:T(8,128)(2,1)}, u32[]{:S(2)}) copy-start(bf16[1024,128]{1,0:T(8,128)(2,1)} %get-tuple-element.13) | copy-start | bytes 786436
  33.9 1.0 %copy-start = (bf16[1024,128]{1,0:T(8,128)(2,1)S(1)}, bf16[1024,128]{1,0:T(8,128)(2,1)}, u32[]{:S(2)}) copy-start(bf16[1024,128]{1,0:T(8,128)(2,1)} %get-tuple-element.14) | copy-start | bytes 786436

commit v2 on v1

--- a/solution.py
+++ b/solution.py
@@ -22,13 +22,12 @@
 
 def kernel(
     n, m, rows,
-    q_hbm, k_hbm, v_hbm, gate_hbm, ct_hbm, decay_ref, gain_ref, state_ref, regroup,
-    go_out, gq_out, gk_out, gv_out, gg_out,
-    q, k, v, gate, ct,
+    q_hbm, k_hbm, v_hbm, gate_hbm, ct_hbm, decay_hbm, gain_hbm, state_hbm, regroup_hbm,
+    go, gq, gk, gv, gg,
+    q, k, v, gate, ct, decay_ref, gain_ref, state_ref, regroup,
     cum_b, rise_b, tail_b, mask, probs, att, scaled, gated, grad, qr, gk_acc, gv_acc,
-    go, gq, gk, gv, gg,
     tots, swap_out, swap_in, f_out, f_in, b_out, b_in, stat, a_out, a_in, start_state,
-    in_sem, out_sem, tot_send, tot_recv, swap_send, swap_recv,
+    in_sem, tot_send, tot_recv, swap_send, swap_recv,
     f_send, f_recv, b_send, b_recv, h_send, h_recv, a_send, a_recv,
 ):
     me = lax.axis_index("ctx")
@@ -45,11 +44,15 @@
     loads = [
         pltpu.make_async_copy(src, dst, in_sem.at[i])
         for i, (src, dst) in enumerate(
-            [(k_hbm, k), (v_hbm, v), (q_hbm, q), (gate_hbm, gate), (ct_hbm, ct)]
+            [
+                (k_hbm, k), (v_hbm, v), (q_hbm, q), (gate_hbm, gate), (ct_hbm, ct),
+                (decay_hbm, decay_ref), (gain_hbm, gain_ref), (state_hbm, state_ref),
+                (regroup_hbm, regroup),
+            ]
         )
     ]
-    for load in loads:
-        load.start()
+    for i in (5, 0, 1, 2, 3, 4, 6, 7, 8):
+        loads[i].start()
 
     barrier = pltpu.get_barrier_semaphore()
 
@@ -71,6 +74,7 @@
     row_i = lax.broadcasted_iota(jnp.int32, (T, T), 0)
     col_i = lax.broadcasted_iota(jnp.int32, (T, T), 1)
     upper = (row_i <= col_i).astype(F32)
+    loads[5].wait()
     partial_sums = lax.dot_general(
         decay_ref[...], upper, NN, precision=lax.Precision.HIGHEST, preferred_element_type=F32
     )
@@ -175,7 +179,8 @@
         att[a * T : w, :] = dot(probs[a * T : w, :w], v[:w, :], NN)
     qr[...] = (q[...].astype(F32) * rise_b[...]).astype(BF16)
     loads[3].wait()
-    loads[4].wait()
+    for i in (4, 6, 7, 8):
+        loads[i].wait()
     on = jax.nn.sigmoid(gate[...].astype(F32))
     scaled[...] = ct[...].astype(F32) * on * gain_ref[...]
 
@@ -289,14 +294,6 @@
 
     lax.fori_loop(1, n, a_go, 0)
     a_in[me] = wanted(me)
-
-    stores = [
-        pltpu.make_async_copy(src, dst, out_sem.at[i])
-        for i, (src, dst) in enumerate(
-            [(go, go_out), (gq, gq_out), (gk, gk_out), (gv, gv_out), (gg, gg_out)]
-        )
-    ]
-    stores[4].start()
 
     for a in range(nb):
         w = (a + 1) * T
@@ -312,7 +309,6 @@
             gv_acc[: a * T, :] += dv[: a * T]
         gk_acc[sl, :] = dk[a * T :]
         gv_acc[sl, :] = dv[a * T :]
-    stores[1].start()
 
     def b_join(o, state):
         i = chips - 1 - o
@@ -322,9 +318,7 @@
     after = lax.fori_loop(0, chips - 1 - chip, b_join, jnp.zeros((T, T), F32))
     after = jnp.where(is_late, after, jnp.exp(tot_row(mate)) * after + other_b).astype(BF16)
     gk[...] = (gk_acc[...] + tail_b[...] * dot(v[...], after, NT)).astype(BF16)
-    stores[2].start()
     gv[...] = (gv_acc[...] + tail_b[...] * dot(k[...], after, NN)).astype(BF16)
-    stores[3].start()
 
     def a_wait(o, c):
         i = lax.rem(me + o, n)
@@ -335,7 +329,6 @@
     for s in range(n):
         src = lax.shift_right_logical(regroup[me * n + s], shift)
         go[s * piece : (s + 1) * piece, :] = a_in[src]
-    stores[0].start()
 
     swap_copy(0).wait_send()
     swap_copy(1).wait_send()
@@ -366,8 +359,17 @@
         return c
 
     lax.fori_loop(0, chip, end_b, 0)
-    for store in stores:
-        store.wait()
+
+
+def store(*refs):
+    sem = refs[-1]
+    copies = [
+        pltpu.make_async_copy(refs[i], refs[5 + i], sem.at[i]) for i in range(5)
+    ]
+    for copy in copies:
+        copy.start()
+    for copy in copies:
+        copy.wait()
 
 
 def per_device(n, m, query, key, value, gate, decay, gain, state_in, cotangent, regroup):
@@ -378,21 +380,24 @@
     big = lambda kind: pltpu.VMEM((rows, T), kind)
     dma = pltpu.SemaphoreType.DMA
     hbm = pl.BlockSpec(memory_space=pl.ANY)
+    any_space = pl.BlockSpec(memory_space=pltpu.HBM)
     vmem = pl.BlockSpec(memory_space=pltpu.VMEM)
-    smem = pl.BlockSpec(memory_space=pltpu.SMEM)
-    return pl.pallas_call(
+    results = pl.pallas_call(
         functools.partial(kernel, n, m, rows),
         out_shape=[jax.ShapeDtypeStruct((rows, T), BF16)] * 5,
-        in_specs=[hbm] * 5 + [vmem] * 3 + [smem],
-        out_specs=[hbm] * 5,
+        in_specs=[any_space] * 9,
+        out_specs=[vmem] * 5,
         scratch_shapes=[big(BF16)] * 5
+        + [
+            pltpu.VMEM((nb, T), F32), pltpu.VMEM((1, T), F32), pltpu.VMEM((1, T, T), F32),
+            pltpu.SMEM((n * n,), jnp.int32),
+        ]
         + [big(F32)] * 3
         + [
             pltpu.VMEM((rows, rows), F32),
             pltpu.VMEM((rows, rows), BF16),
             big(F32), big(F32), pltpu.VMEM((n, piece, T), BF16), big(BF16), big(BF16), big(F32), big(F32),
         ]
-        + [big(BF16)] * 5
         + [
             pltpu.VMEM((n, 8, T), F32),
             pltpu.VMEM((2, T, T), F32),
@@ -407,18 +412,32 @@
             pltpu.VMEM((T, T), BF16),
         ]
         + [
-            dma((5,)), dma((5,)), dma((n,)), dma((n,)), dma((2,)), dma((2,)),
+            dma((9,)), dma((n,)), dma((n,)), dma((2,)), dma((2,)),
             dma((chips,)), dma((chips,)), dma((chips,)), dma((chips,)),
             dma((m,)), dma((m,)), dma((n,)), dma((n,)),
         ],
         compiler_params=pltpu.CompilerParams(
-            collective_id=0, has_side_effects=True, vmem_limit_bytes=62 << 20
+            collective_id=0, has_side_effects=True, vmem_limit_bytes=40 << 20
         ),
         name="layer",
     )(
-        query, key, value, gate, cotangent,
-        decay.reshape((nb, T)), gain.reshape((1, T)), state_in, regroup,
+        *[
+            pltpu.with_memory_space_constraint(x, pltpu.HBM)
+            for x in (
+                query, key, value, gate, cotangent,
+                decay.reshape((nb, T)), gain.reshape((1, T)), state_in, regroup,
+            )
+        ]
     )
+    return pl.pallas_call(
+        store,
+        out_shape=[jax.ShapeDtypeStruct((rows, T), BF16)] * 5,
+        in_specs=[hbm] * 5,
+        out_specs=[any_space] * 5,
+        scratch_shapes=[dma((5,))],
+        compiler_params=pltpu.CompilerParams(vmem_limit_bytes=1 << 20),
+        name="store",
+    )(*results)
 
 
 def solution(mesh):

time: 36.1 us -> 30.2 us (0.84)
  local copies, waits for them, and re-layouts: 5.55 us -> 0 us
    unnamed x13 -> x0, local copies, waits for them, and re-layouts: 5.55 us -> none
    pallas_call x1, Pallas kernels: 29.5 us -> 28.2 us  [per_device(): pl.pallas_call(functools.partial(kernel, n, m, rows), out_shape=[jax.Shap...]
    pallas_call x0 -> x1, Pallas kernels: none -> 1.09 us  [per_device(): pl.pallas_call(store, out_shape=[jax.ShapeDtypeStruct((rows, T), BF16)] *...]
where the time goes in v2:
time: 30.2 us; the launch traced here: 29.9 us
  Pallas kernels  29.3 us (97%)
  between operations  0.64 us (2%)
    pallas_call x1, Pallas kernels, per_device(): pl.pallas_call(functools.partial(kernel, n, m, rows), out_shape=[jax.Shap...  28.2 us
    pallas_call x1, Pallas kernels, per_device(): pl.pallas_call(store, out_shape=[jax.ShapeDtypeStruct((rows, T), BF16)] *...  1.09 us

profile of v2, /device:TPU:0, one launch (start us, length us, event | category | flops | bytes accessed | tf_op | source)
XLA Modules:
  0.0 29.9 jit_solution(8162411040089350066)
XLA Ops:
  0.6 28.2 %layer.1 = (bf16[1024,128]{1,0:T(8,128)(2,1)S(1)}, bf16[1024,128]{1,0:T(8,128)(2,1)S(1)}, bf16[1024,128]{1,0:T(8,128)(2,1)S(1)}, bf16[1024,128]{1,0:T(8,128)(2,1)S(1)}, bf16[1024,128]{1,0:T(8,128)(2,1)S(1)}) custom-call(bf16[1024,128]{1,0:T(8,128)(2,1)} %q_hbm.1, bf16[1024,128]{1,0:T(8,128)(2,1)} %k_hbm.1, bf16[1024,128]{1,0:T(8,128)(2,1)} %v_hbm.1, ...), custom_call_target="tpu_custom_call" | custom-call | tf_op jit(solution)/shard_map/layer/pallas_call | solution.py:385
  28.8 1.1 %store.1 = (bf16[1024,128]{1,0:T(8,128)(2,1)}, bf16[1024,128]{1,0:T(8,128)(2,1)}, bf16[1024,128]{1,0:T(8,128)(2,1)}, bf16[1024,128]{1,0:T(8,128)(2,1)}, bf16[1024,128]{1,0:T(8,128)(2,1)}) custom-call(bf16[1024,128]{1,0:T(8,128)(2,1)S(1)} %get-tuple-element.10.refs_0_, bf16[1024,128]{1,0:T(8,128)(2,1)S(1)} %get-tuple-element.11.refs_1_, ...), custom_call_target="tpu_custom_call" | custom-call | tf_op jit(solution)/shard_map/store/pallas_call | solution.py:432

commit v3 on v2

--- a/solution.py
+++ b/solution.py
@@ -20,15 +20,27 @@
     return lax.dot_general(a, b, dims, preferred_element_type=F32)
 
 
+def columns(rows):
+    filler = jnp.zeros((T - sum(x.shape[0] for x in rows), T), F32)
+    return jnp.transpose(jnp.concatenate([*rows, filler], axis=0))
+
+
+def row_sums(x):
+    high = x.astype(BF16)
+    low = (x - high.astype(F32)).astype(BF16)
+    ones = jnp.ones((8, T), BF16)
+    return dot(ones, high, NT) + dot(ones, low, NT)
+
+
 def kernel(
     n, m, rows,
     q_hbm, k_hbm, v_hbm, gate_hbm, ct_hbm, decay_hbm, gain_hbm, state_hbm, regroup_hbm,
     go, gq, gk, gv, gg,
     q, k, v, gate, ct, decay_ref, gain_ref, state_ref, regroup,
     cum_b, rise_b, tail_b, mask, probs, att, scaled, gated, grad, qr, gk_acc, gv_acc,
-    tots, swap_out, swap_in, f_out, f_in, b_out, b_in, stat, a_out, a_in, start_state,
+    tots, swap_out, swap_in, f_out, f_in, b_out, b_in, stat, a_out, a_in, start_state, inv_rows, inv_part, picks,
     in_sem, tot_send, tot_recv, swap_send, swap_recv,
-    f_send, f_recv, b_send, b_recv, h_send, h_recv, a_send, a_recv,
+    f_send, f_recv, b_send, b_recv, h_send, h_recv, a_send, a_recv, i_send, i_recv,
 ):
     me = lax.axis_index("ctx")
     head = lax.axis_index("head")
@@ -86,9 +98,10 @@
         offset = offset + row[:, T - 1 : T]
     total = jnp.broadcast_to(crow[-1][:, T - 1 : T], (1, T))
     tots[pl.ds(me, 1)] = jnp.broadcast_to(total, (8, T))[None]
+    cols = columns(crow)
     for r in range(nb):
         sl = slice(r * T, (r + 1) * T)
-        cb = jnp.transpose(jnp.broadcast_to(crow[r], (T, T)))
+        cb = jnp.broadcast_to(cols[:, r : r + 1], (T, T))
         cum_b[sl, :] = cb
         rise_b[sl, :] = jnp.exp(cb)
         tail_b[sl, :] = jnp.exp(total - cb)
@@ -145,11 +158,12 @@
         scores_for(a)
 
     def tot_wait(o, c):
-        tot_copy(lax.rem(me + o, n), lax.rem(me + o, n)).wait_recv()
-        return c
-
-    lax.fori_loop(1, n, tot_wait, 0)
+        i = lax.rem(2 * chip + o, n)
+        tot_copy(i, i).wait_recv()
+        return c
+
     swap_copy(0).wait_recv()
+    tot_copy(mate, mate).wait_recv()
 
     def tot_row(i):
         return tots[pl.ds(i, 1)][0, 0:1, :]
@@ -177,13 +191,27 @@
     for a in range(nb):
         w = (a + 1) * T
         att[a * T : w, :] = dot(probs[a * T : w, :w], v[:w, :], NN)
-    qr[...] = (q[...].astype(F32) * rise_b[...]).astype(BF16)
+    qr[...] = jnp.transpose((q[...].astype(F32) * rise_b[...]).astype(BF16))
     loads[3].wait()
     for i in (4, 6, 7, 8):
         loads[i].wait()
     on = jax.nn.sigmoid(gate[...].astype(F32))
     scaled[...] = ct[...].astype(F32) * on * gain_ref[...]
 
+    def pick(d):
+        def one(s, found):
+            p = regroup[d * n + s]
+            apart = lax.shift_right_logical(p, shift) - me
+            return found + (1 - jnp.minimum(apart * apart, 1)) * (p & (n - 1))
+
+        return lax.fori_loop(0, n, one, jnp.int32(0), unroll=8)
+
+    def pick_store(d, c):
+        picks[d] = pick(d)
+        return c
+
+    lax.fori_loop(0, n, pick_store, 0)
+
     def chip_total(i):
         return tot_row(2 * i) + tot_row(2 * i + 1)
 
@@ -191,6 +219,7 @@
         f_copy(i, i).wait_recv()
         return jnp.exp(chip_total(i)) * state + f_in[pl.ds(i, 1)][0].astype(F32)
 
+    lax.fori_loop(2, n, tot_wait, 0)
     state = lax.fori_loop(0, chip, f_join, state_ref[0])
     state = jnp.where(is_late, jnp.exp(tot_row(mate)) * state + other, state)
     start_state[...] = state.astype(BF16)
@@ -199,12 +228,10 @@
         sl = slice(r * T, (r + 1) * T)
         flat = att[sl, :] + rise_b[sl, :] * dot(q[sl, :], start_state[...], NN)
         att[sl, :] = flat
-        stat[pl.ds(head, 1), r : r + 1, :] = jnp.sum(
-            jnp.transpose(flat * flat), axis=0, keepdims=True
-        )[None]
-        stat[pl.ds(head, 1), nb + r : nb + r + 1, :] = jnp.sum(
-            jnp.transpose(flat * scaled[sl, :]), axis=0, keepdims=True
-        )[None]
+        squares = row_sums(flat * flat)[0:1]
+        cross = row_sums(flat * scaled[sl, :])[0:1]
+        stat[pl.ds(head, 1), r : r + 1, :] = squares[None]
+        stat[pl.ds(head, 1), nb + r : nb + r + 1, :] = cross[None]
 
     def h_copy(slot, to):
         return pltpu.make_async_remote_copy(
@@ -218,6 +245,33 @@
         return c
 
     lax.fori_loop(1, m, h_go, 0)
+
+    per_tile = T // piece
+    for r in range(nb):
+        sl = slice(r * T, (r + 1) * T)
+        on = jax.nn.sigmoid(gate[sl, :].astype(F32))
+        out = (att[sl, :] * gain_ref[...] * on).astype(BF16)
+        for part in range(per_tile):
+            gated[r * per_tile + part] = out[part * piece : (part + 1) * piece]
+
+    def wanted(d):
+        return gated[picks[d]]
+
+    def a_copy(slot, to):
+        return pltpu.make_async_remote_copy(
+            src_ref=a_out.at[to], dst_ref=a_in.at[slot],
+            send_sem=a_send.at[to], recv_sem=a_recv.at[slot],
+            device_id={"ctx": to}, device_id_type=MESH,
+        )
+
+    def a_go(o, c):
+        to = lax.rem(me + o, n)
+        a_out[to] = wanted(to)
+        a_copy(me, to).start()
+        return c
+
+    lax.fori_loop(1, n, a_go, 0)
+    a_in[me] = wanted(me)
 
     def h_join(o, acc):
         i = lax.rem(head + o, m)
@@ -227,25 +281,38 @@
     sums = lax.fori_loop(1, m, h_join, stat[pl.ds(head, 1)][0])
     inv = lax.rsqrt(sums[:nb] / width_all + 1e-06)
     coef = inv * inv * inv * sums[nb:] / width_all
+    inv_rows[pl.ds(me, 1)] = inv[None]
+    cols = columns([inv, coef])
     for r in range(nb):
         sl = slice(r * T, (r + 1) * T)
-        inv_b = jnp.transpose(jnp.broadcast_to(inv[r : r + 1, :], (T, T)))
-        coef_b = jnp.transpose(jnp.broadcast_to(coef[r : r + 1, :], (T, T)))
+        inv_b = jnp.broadcast_to(cols[:, r : r + 1], (T, T))
+        coef_b = jnp.broadcast_to(cols[:, nb + r : nb + r + 1], (T, T))
         flat = att[sl, :]
         grad[sl, :] = (inv_b * scaled[sl, :] - flat * coef_b).astype(BF16)
-        att[sl, :] = flat * inv_b * gain_ref[...]
-
-    back = dot(qr[...], grad[...], TN)
+        att[sl, :] = flat * inv_b
+
+    back = dot(qr[...], grad[...], NN)
     swap_out[1] = back
     swap_copy(1).start()
+
+    def i_copy(slot, to):
+        return pltpu.make_async_remote_copy(
+            src_ref=inv_rows.at[me], dst_ref=inv_rows.at[slot],
+            send_sem=i_send.at[to], recv_sem=i_recv.at[slot],
+            device_id={"ctx": to}, device_id_type=MESH,
+        )
+
+    def i_go(o, c):
+        to = lax.rem(me + o, n)
+        i_copy(me, to).start()
+        return c
+
+    lax.fori_loop(1, n, i_go, 0)
 
     for r in range(nb):
         sl = slice(r * T, (r + 1) * T)
         on = jax.nn.sigmoid(gate[sl, :].astype(F32))
-        normed = att[sl, :]
-        out = (normed * on).astype(BF16)
-        for part in range(T // piece):
-            gated[r * (T // piece) + part] = out[part * piece : (part + 1) * piece]
+        normed = att[sl, :] * gain_ref[...]
         gg[sl, :] = (ct[sl, :].astype(F32) * normed * on * (1.0 - on)).astype(BF16)
 
     swap_copy(1).wait_recv()
@@ -267,33 +334,6 @@
         return c
 
     lax.fori_loop(0, chip, b_go, 0)
-
-    def pick(d):
-        def one(s, found):
-            p = regroup[d * n + s]
-            apart = lax.shift_right_logical(p, shift) - me
-            return found + (1 - jnp.minimum(apart * apart, 1)) * (p & (n - 1))
-
-        return lax.fori_loop(0, n, one, jnp.int32(0), unroll=8)
-
-    def wanted(d):
-        return gated[pick(d)]
-
-    def a_copy(slot, to):
-        return pltpu.make_async_remote_copy(
-            src_ref=a_out.at[to], dst_ref=a_in.at[slot],
-            send_sem=a_send.at[to], recv_sem=a_recv.at[slot],
-            device_id={"ctx": to}, device_id_type=MESH,
-        )
-
-    def a_go(o, c):
-        to = lax.rem(me + o, n)
-        a_out[to] = wanted(to)
-        a_copy(me, to).start()
-        return c
-
-    lax.fori_loop(1, n, a_go, 0)
-    a_in[me] = wanted(me)
 
     for a in range(nb):
         w = (a + 1) * T
@@ -310,6 +350,32 @@
         gk_acc[sl, :] = dk[a * T :]
         gv_acc[sl, :] = dv[a * T :]
 
+    def a_wait(o, c):
+        i = lax.rem(me + o, n)
+        a_copy(i, i).wait_recv()
+        i_copy(i, i).wait_recv()
+        return c
+
+    lax.fori_loop(1, n, a_wait, 0)
+    lane_row = lax.broadcasted_iota(jnp.int32, (nb, T), 0)
+    chosen = []
+    for s in range(n):
+        p = regroup[me * n + s]
+        apart = lane_row - lax.shift_right_logical(p & (n - 1), per_tile.bit_length() - 1)
+        here = (1 - jnp.minimum(apart * apart, 1)).astype(F32)
+        tile = inv_rows[lax.shift_right_logical(p, shift)]
+        chosen.append(jnp.sum(tile * here, axis=0, keepdims=True))
+    cols = columns(chosen)
+    for s in range(n):
+        p = regroup[me * n + s]
+        inv_b = jnp.broadcast_to(cols[:, s : s + 1], (T, T))
+        if per_tile > 1:
+            for part in range(per_tile):
+                inv_part[part] = inv_b[part * piece : (part + 1) * piece]
+            inv_b = inv_part[p & (per_tile - 1)]
+        arrived = a_in[lax.shift_right_logical(p, shift)].astype(F32)
+        go[s * piece : (s + 1) * piece, :] = (arrived * inv_b).astype(BF16)
+
     def b_join(o, state):
         i = chips - 1 - o
         b_copy(i, i).wait_recv()
@@ -320,16 +386,6 @@
     gk[...] = (gk_acc[...] + tail_b[...] * dot(v[...], after, NT)).astype(BF16)
     gv[...] = (gv_acc[...] + tail_b[...] * dot(k[...], after, NN)).astype(BF16)
 
-    def a_wait(o, c):
-        i = lax.rem(me + o, n)
-        a_copy(i, i).wait_recv()
-        return c
-
-    lax.fori_loop(1, n, a_wait, 0)
-    for s in range(n):
-        src = lax.shift_right_logical(regroup[me * n + s], shift)
-        go[s * piece : (s + 1) * piece, :] = a_in[src]
-
     swap_copy(0).wait_send()
     swap_copy(1).wait_send()
 
@@ -337,6 +393,7 @@
         to = lax.rem(me + o, n)
         tot_copy(to, to).wait_send()
         a_copy(to, to).wait_send()
+        i_copy(to, to).wait_send()
         return c
 
     lax.fori_loop(1, n, end_ctx, 0)
@@ -396,7 +453,7 @@
         + [
             pltpu.VMEM((rows, rows), F32),
             pltpu.VMEM((rows, rows), BF16),
-            big(F32), big(F32), pltpu.VMEM((n, piece, T), BF16), big(BF16), big(BF16), big(F32), big(F32),
+            big(F32), big(F32), pltpu.VMEM((n, piece, T), BF16), big(BF16), pltpu.VMEM((T, rows), BF16), big(F32), big(F32),
         ]
         + [
             pltpu.VMEM((n, 8, T), F32),
@@ -410,11 +467,14 @@
             pltpu.VMEM((n, piece, T), BF16),
             pltpu.VMEM((n, piece, T), BF16),
             pltpu.VMEM((T, T), BF16),
+            pltpu.VMEM((n, nb, T), F32),
+            pltpu.VMEM((T // piece, piece, T), F32),
+            pltpu.SMEM((n,), jnp.int32),
         ]
         + [
             dma((9,)), dma((n,)), dma((n,)), dma((2,)), dma((2,)),
             dma((chips,)), dma((chips,)), dma((chips,)), dma((chips,)),
-            dma((m,)), dma((m,)), dma((n,)), dma((n,)),
+            dma((m,)), dma((m,)), dma((n,)), dma((n,)), dma((n,)), dma((n,)),
         ],
         compiler_params=pltpu.CompilerParams(
             collective_id=0, has_side_effects=True, vmem_limit_bytes=40 << 20

time: 30.2 us -> 25.4 us (0.84)
  Pallas kernels: 29.3 us -> 24.5 us
    pallas_call x1, Pallas kernels: 28.2 us -> 23.5 us  [per_device(): pl.pallas_call(functools.partial(kernel, n, m, rows), out_shape=[jax.Shap...]
where the time goes in v3:
time: 25.4 us; the launch traced here: 25.2 us
  Pallas kernels  24.5 us (96%)
  between operations  0.64 us (3%)
    pallas_call x1, Pallas kernels, per_device(): pl.pallas_call(functools.partial(kernel, n, m, rows), out_shape=[jax.Shap...  23.5 us
    pallas_call x1, Pallas kernels, per_device(): pl.pallas_call(store, out_shape=[jax.ShapeDtypeStruct((rows, T), BF16)] *...  1.09 us

profile of v3, /device:TPU:0, one launch (start us, length us, event | category | flops | bytes accessed | tf_op | source)
XLA Modules:
  0.0 25.2 jit_solution(11571177666630141844)
XLA Ops:
  0.6 23.5 %layer.1 = (bf16[1024,128]{1,0:T(8,128)(2,1)S(1)}, bf16[1024,128]{1,0:T(8,128)(2,1)S(1)}, bf16[1024,128]{1,0:T(8,128)(2,1)S(1)}, bf16[1024,128]{1,0:T(8,128)(2,1)S(1)}, bf16[1024,128]{1,0:T(8,128)(2,1)S(1)}) custom-call(bf16[1024,128]{1,0:T(8,128)(2,1)} %q_hbm.1, bf16[1024,128]{1,0:T(8,128)(2,1)} %k_hbm.1, bf16[1024,128]{1,0:T(8,128)(2,1)} %v_hbm.1, ...), custom_call_target="tpu_custom_call" | custom-call | tf_op jit(solution)/shard_map/layer/pallas_call | solution.py:442
  24.1 1.1 %store.1 = (bf16[1024,128]{1,0:T(8,128)(2,1)}, bf16[1024,128]{1,0:T(8,128)(2,1)}, bf16[1024,128]{1,0:T(8,128)(2,1)}, bf16[1024,128]{1,0:T(8,128)(2,1)}, bf16[1024,128]{1,0:T(8,128)(2,1)}) custom-call(bf16[1024,128]{1,0:T(8,128)(2,1)S(1)} %get-tuple-element.10.refs_0_, bf16[1024,128]{1,0:T(8,128)(2,1)S(1)} %get-tuple-element.11.refs_1_, ...), custom_call_target="tpu_custom_call" | custom-call | tf_op jit(solution)/shard_map/store/pallas_call | solution.py:492

commit v4 on v3

--- a/solution.py
+++ b/solution.py
@@ -37,8 +37,8 @@
     q_hbm, k_hbm, v_hbm, gate_hbm, ct_hbm, decay_hbm, gain_hbm, state_hbm, regroup_hbm,
     go, gq, gk, gv, gg,
     q, k, v, gate, ct, decay_ref, gain_ref, state_ref, regroup,
-    cum_b, rise_b, tail_b, mask, probs, att, scaled, gated, grad, qr, gk_acc, gv_acc,
-    tots, swap_out, swap_in, f_out, f_in, b_out, b_in, stat, a_out, a_in, start_state, inv_rows, inv_part, picks,
+    cum_b, rise_b, tail_b, mask, probs, att, scaled, on_b, gated, grad, qr, gk_acc, gv_acc,
+    tots, swap_out, swap_in, f_out, f_in, b_out, b_in, stat, a_out, a_in, start_state, inv_rows, inv_part, picks, ds, probs_t,
     in_sem, tot_send, tot_recv, swap_send, swap_recv,
     f_send, f_recv, b_send, b_recv, h_send, h_recv, a_send, a_recv, i_send, i_recv,
 ):
@@ -51,6 +51,9 @@
     nb = rows // T
     piece = rows // n
     width_all = m * T
+    per_block = 2
+    G = per_block * T
+    groups = rows // G
     shift = n.bit_length() - 1
 
     loads = [
@@ -97,7 +100,7 @@
         crow.append(row + offset)
         offset = offset + row[:, T - 1 : T]
     total = jnp.broadcast_to(crow[-1][:, T - 1 : T], (1, T))
-    tots[pl.ds(me, 1)] = jnp.broadcast_to(total, (8, T))[None]
+    tots[pl.ds(me, 1)] = total[None]
     cols = columns(crow)
     for r in range(nb):
         sl = slice(r * T, (r + 1) * T)
@@ -141,19 +144,24 @@
 
     def decay_tile(a, b):
         diff = cum_b[a * T : (a + 1) * T, :] - crow[b]
+        if a < b:
+            return jnp.zeros((T, T), F32)
         if a == b:
             return jnp.where(causal, jnp.exp(jnp.where(causal, diff, 0.0)), 0.0)
         return jnp.exp(diff)
 
-    def scores_for(a):
-        w = (a + 1) * T
-        s = dot(q[a * T : w, :], k[:w, :], NT)
-        for b in range(a + 1):
-            d = decay_tile(a, b)
-            mask[a * T : w, b * T : (b + 1) * T] = d
-            probs[a * T : w, b * T : (b + 1) * T] = (s[:, b * T : (b + 1) * T] * d).astype(BF16)
-
-    half = nb // 4
+    def scores_for(g):
+        w = (g + 1) * G
+        s = dot(q[g * G : w, :], k[:w, :], NT)
+        for a in range(g * per_block, (g + 1) * per_block):
+            up = a * T - g * G
+            for b in range(w // T):
+                at = (slice(a * T, (a + 1) * T), slice(b * T, (b + 1) * T))
+                d = decay_tile(a, b)
+                mask[at] = d
+                probs[at] = (s[up : up + T, b * T : (b + 1) * T] * d).astype(BF16)
+
+    half = groups // 2
     for a in range(half):
         scores_for(a)
 
@@ -166,7 +174,7 @@
     tot_copy(mate, mate).wait_recv()
 
     def tot_row(i):
-        return tots[pl.ds(i, 1)][0, 0:1, :]
+        return tots[pl.ds(i, 1)][0]
 
     mine, other = swap_out[0], swap_in[0]
     is_late = core == 1
@@ -186,17 +194,16 @@
 
     lax.fori_loop(chip + 1, chips, f_go, 0)
 
-    for a in range(half, nb):
+    for a in range(half, groups):
         scores_for(a)
-    for a in range(nb):
-        w = (a + 1) * T
-        att[a * T : w, :] = dot(probs[a * T : w, :w], v[:w, :], NN)
-    qr[...] = jnp.transpose((q[...].astype(F32) * rise_b[...]).astype(BF16))
+    for g in range(groups):
+        w = (g + 1) * G
+        att[g * G : w, :] = dot(probs[g * G : w, :w], v[:w, :], NN)
     loads[3].wait()
     for i in (4, 6, 7, 8):
         loads[i].wait()
-    on = jax.nn.sigmoid(gate[...].astype(F32))
-    scaled[...] = ct[...].astype(F32) * on * gain_ref[...]
+    on_b[...] = jax.nn.sigmoid(gate[...].astype(F32))
+    scaled[...] = ct[...].astype(F32) * on_b[...] * gain_ref[...]
 
     def pick(d):
         def one(s, found):
@@ -209,8 +216,6 @@
     def pick_store(d, c):
         picks[d] = pick(d)
         return c
-
-    lax.fori_loop(0, n, pick_store, 0)
 
     def chip_total(i):
         return tot_row(2 * i) + tot_row(2 * i + 1)
@@ -246,10 +251,11 @@
 
     lax.fori_loop(1, m, h_go, 0)
 
+    lax.fori_loop(0, n, pick_store, 0)
     per_tile = T // piece
     for r in range(nb):
         sl = slice(r * T, (r + 1) * T)
-        on = jax.nn.sigmoid(gate[sl, :].astype(F32))
+        on = on_b[sl, :]
         out = (att[sl, :] * gain_ref[...] * on).astype(BF16)
         for part in range(per_tile):
             gated[r * per_tile + part] = out[part * piece : (part + 1) * piece]
@@ -272,6 +278,11 @@
 
     lax.fori_loop(1, n, a_go, 0)
     a_in[me] = wanted(me)
+
+    qr[...] = jnp.transpose((q[...].astype(F32) * rise_b[...]).astype(BF16))
+    for g in range(groups):
+        sl = slice(g * G, (g + 1) * G)
+        probs_t[sl, g * G :] = jnp.transpose(probs[g * G :, sl])
 
     def h_join(o, acc):
         i = lax.rem(head + o, m)
@@ -311,7 +322,7 @@
 
     for r in range(nb):
         sl = slice(r * T, (r + 1) * T)
-        on = jax.nn.sigmoid(gate[sl, :].astype(F32))
+        on = on_b[sl, :]
         normed = att[sl, :] * gain_ref[...]
         gg[sl, :] = (ct[sl, :].astype(F32) * normed * on * (1.0 - on)).astype(BF16)
 
@@ -335,20 +346,18 @@
 
     lax.fori_loop(0, chip, b_go, 0)
 
-    for a in range(nb):
-        w = (a + 1) * T
-        sl = slice(a * T, w)
-        ds = (dot(grad[sl, :], v[:w, :], NT) * mask[sl, :w]).astype(BF16)
+    for g in range(groups):
+        w = (g + 1) * G
+        sl = slice(g * G, w)
+        ds[sl, :w] = (dot(grad[sl, :], v[:w, :], NT) * mask[sl, :w]).astype(BF16)
         gq[sl, :] = (
-            dot(ds, k[:w, :], NN) + rise_b[sl, :] * dot(grad[sl, :], start_state[...], NT)
+            dot(ds[sl, :w], k[:w, :], NN)
+            + rise_b[sl, :] * dot(grad[sl, :], start_state[...], NT)
         ).astype(BF16)
-        dk = dot(ds, q[sl, :], TN)
-        dv = dot(probs[sl, :w], grad[sl, :], TN)
-        if a:
-            gk_acc[: a * T, :] += dk[: a * T]
-            gv_acc[: a * T, :] += dv[: a * T]
-        gk_acc[sl, :] = dk[a * T :]
-        gv_acc[sl, :] = dv[a * T :]
+    for g in range(groups):
+        sl = slice(g * G, (g + 1) * G)
+        gk_acc[sl, :] = dot(ds[g * G :, sl], q[g * G :, :], TN)
+        gv_acc[sl, :] = dot(probs_t[sl, g * G :], grad[g * G :, :], NN)
 
     def a_wait(o, c):
         i = lax.rem(me + o, n)
@@ -453,10 +462,10 @@
         + [
             pltpu.VMEM((rows, rows), F32),
             pltpu.VMEM((rows, rows), BF16),
-            big(F32), big(F32), pltpu.VMEM((n, piece, T), BF16), big(BF16), pltpu.VMEM((T, rows), BF16), big(F32), big(F32),
+            big(F32), big(F32), big(F32), pltpu.VMEM((n, piece, T), BF16), big(BF16), pltpu.VMEM((T, rows), BF16), big(F32), big(F32),
         ]
         + [
-            pltpu.VMEM((n, 8, T), F32),
+            pltpu.VMEM((n, 1, T), F32),
             pltpu.VMEM((2, T, T), F32),
             pltpu.VMEM((2, T, T), F32),
             pltpu.VMEM((T, T), BF16),
@@ -470,6 +479,8 @@
             pltpu.VMEM((n, nb, T), F32),
             pltpu.VMEM((T // piece, piece, T), F32),
             pltpu.SMEM((n,), jnp.int32),
+            pltpu.VMEM((rows, rows), BF16),
+            pltpu.VMEM((rows, rows), BF16),
         ]
         + [
             dma((9,)), dma((n,)), dma((n,)), dma((2,)), dma((2,)),

time: 25.4 us -> 25.3 us (level)
  no operation moved by 1% of the time
where the time goes in v4:
time: 25.3 us; the launch traced here: 25.2 us
  Pallas kernels  24.5 us (97%)
  between operations  0.64 us (3%)
    pallas_call x1, Pallas kernels, per_device(): pl.pallas_call(functools.partial(kernel, n, m, rows), out_shape=[jax.Shap...  23.4 us
    pallas_call x1, Pallas kernels, per_device(): pl.pallas_call(store, out_shape=[jax.ShapeDtypeStruct((rows, T), BF16)] *...  1.09 us

profile of v4, /device:TPU:0, one launch (start us, length us, event | category | flops | bytes accessed | tf_op | source)
XLA Modules:
  0.0 25.2 jit_solution(2670129556420630217)
XLA Ops:
  0.6 23.4 %layer.1 = (bf16[1024,128]{1,0:T(8,128)(2,1)S(1)}, bf16[1024,128]{1,0:T(8,128)(2,1)S(1)}, bf16[1024,128]{1,0:T(8,128)(2,1)S(1)}, bf16[1024,128]{1,0:T(8,128)(2,1)S(1)}, bf16[1024,128]{1,0:T(8,128)(2,1)S(1)}) custom-call(bf16[1024,128]{1,0:T(8,128)(2,1)} %q_hbm.1, bf16[1024,128]{1,0:T(8,128)(2,1)} %k_hbm.1, bf16[1024,128]{1,0:T(8,128)(2,1)} %v_hbm.1, ...), custom_call_target="tpu_custom_call" | custom-call | tf_op jit(solution)/shard_map/layer/pallas_call | solution.py:451
  24.1 1.1 %store.1 = (bf16[1024,128]{1,0:T(8,128)(2,1)}, bf16[1024,128]{1,0:T(8,128)(2,1)}, bf16[1024,128]{1,0:T(8,128)(2,1)}, bf16[1024,128]{1,0:T(8,128)(2,1)}, bf16[1024,128]{1,0:T(8,128)(2,1)}) custom-call(bf16[1024,128]{1,0:T(8,128)(2,1)S(1)} %get-tuple-element.10.refs_0_, bf16[1024,128]{1,0:T(8,128)(2,1)S(1)} %get-tuple-element.11.refs_1_, ...), custom_call_target="tpu_custom_call" | custom-call | tf_op jit(solution)/shard_map/store/pallas_call | solution.py:503
